TPU v7x, 32 devices: a whole 2x2x4 slice. The times are simulated.
32 devices in a mesh: group: 4 (over y, core), dom: 8 (over z, x).
Axes of the slice: x: 2, y: 2, z: 4, core: 2. Of those that a mesh axis runs over, the one named last changes fastest.
Arguments:
- features: float32 [4096, 1024], P(('group', 'dom')), may hold values from -6 to 6
- known_mask: int32 [4096], P(('group', 'dom')), may hold values 0 or 1
- local_tile: bfloat16 [4096, 128], P(('group', 'dom')), may hold values from 0 to 1.5, as said below
- peer_tile: bfloat16 [4096, 256], P(('group', 'dom')), may hold values from 0 to 1.5, as said below
- cross_tile: bfloat16 [4096, 128], P(('group', 'dom')), may hold values from 0 to 1.5, as said below
- peer_rows: int32 [4, 8, 8, 32], P('group', 'dom'), may hold values from 0 to 127
- cross_rows: int32 [4, 8, 4, 32], P('group', 'dom'), may hold values from 0 to 127
- labels: int32 [4096], P(('group', 'dom')), may hold values from 0 to 18
- first_weight: bfloat16 [1024, 1024], replicated, may hold values from -0.1875 to 0.1875
- first_bias: float32 [1024], replicated, may hold values from -3 to 3
- second_weight: bfloat16 [1024, 19], replicated, may hold values from -60 to 60
- second_bias: float32 [19], replicated, may hold values from -3 to 3
Outputs:
- imputed: float32 [4096, 1024], P(('group', 'dom'))
- grad_first: float32 [1024, 1024], P('dom')
- grad_first_bias: float32 [1024], replicated
- grad_second: float32 [1024, 19], replicated
- grad_second_bias: float32 [19], replicated
Inputs may be any that keep to these rules, and one draw needn't show every extreme that they name: `local_tile`: each entry is 0 or lies in 0.5 to 1.5; a fraction of about 8 / 128 is nonzero. `peer_tile`: each entry is 0 or lies in 0.5 to 1.5; a fraction of about 6 / 256 is nonzero. `cross_tile`: each entry is 0 or lies in 0.5 to 1.5; a fraction of about 4 / 128 is nonzero.
All inputs are finite; a program needn't handle non-finite values. No bound on the sum of `known_mask` on one device may be relied on, other than what follows from the above.
Results may differ from a plain program's by a relative error of at most 0.0041.
Values sent between devices are 32-bit elements; how exact they have to be, the bound alone decides.
A program may use at most 64 MiB of HBM per device.

v0:
```python
import math
import jax
import jax.numpy as jnp
from jax import lax
from jax.sharding import PartitionSpec as P

SWEEPS = 3


def fetch_halos(current, peer_list, cross_list):
    width = current.shape[1]
    outgoing = current[peer_list.reshape(-1)].reshape(peer_list.shape[2], peer_list.shape[3], width)
    incoming = lax.all_to_all(outgoing, "dom", split_axis=0, concat_axis=0, tiled=True)
    leaving = current[cross_list.reshape(-1)].reshape(
        cross_list.shape[2], cross_list.shape[3], width
    )
    arriving = lax.all_to_all(leaving, "group", split_axis=0, concat_axis=0, tiled=True)
    return (incoming.reshape(-1, width), arriving.reshape(-1, width))


def local(
    features,
    known_mask,
    local_tile,
    peer_tile,
    cross_tile,
    peer_rows,
    cross_rows,
    labels,
    first_weight,
    first_bias,
    second_weight,
    second_bias,
):
    highest = lax.Precision.HIGHEST
    keep = (known_mask == 1)[:, None]
    current = jnp.where(keep, features, jnp.float32(0.0))
    local_full = local_tile.astype(jnp.float32)
    peer_full = peer_tile.astype(jnp.float32)
    cross_full = cross_tile.astype(jnp.float32)
    degree = (
        1.0 + jnp.sum(local_full, axis=1) + jnp.sum(peer_full, axis=1) + jnp.sum(cross_full, axis=1)
    )
    degree = degree[:, None]
    for sweep in range(SWEEPS):
        incoming, arriving = fetch_halos(current, peer_rows, cross_rows)
        summed = current + jnp.dot(
            local_full, current, precision=highest, preferred_element_type=jnp.float32
        )
        summed = summed + jnp.dot(
            peer_full, incoming, precision=highest, preferred_element_type=jnp.float32
        )
        summed = summed + jnp.dot(
            cross_full, arriving, precision=highest, preferred_element_type=jnp.float32
        )
        current = jnp.where(keep, features, summed / degree)
    inputs = current.astype(jnp.bfloat16)
    pre = jnp.dot(inputs, first_weight, preferred_element_type=jnp.float32) + first_bias
    sigma = jax.nn.sigmoid(pre)
    active = (pre * sigma).astype(jnp.bfloat16)
    logits = jnp.dot(active, second_weight, preferred_element_type=jnp.float32) + second_bias
    shifted = logits - jnp.max(logits, axis=1, keepdims=True)
    expo = jnp.exp(shifted)
    probs = expo / jnp.sum(expo, axis=1, keepdims=True)
    classes = second_weight.shape[1]
    onehot = (labels[:, None] == jnp.arange(classes, dtype=jnp.int32)[None, :]).astype(jnp.float32)
    total_nodes = features.shape[0] * lax.axis_size("group") * lax.axis_size("dom")
    dlogits = (probs - onehot) / jnp.float32(math.sqrt(total_nodes))
    dlogits_b = dlogits.astype(jnp.bfloat16)
    second_bias_term = jnp.sum(dlogits, axis=0)
    second_term = lax.dot_general(
        active, dlogits_b, (((0,), (0,)), ((), ())), preferred_element_type=jnp.float32
    )
    back = lax.dot_general(
        dlogits_b, second_weight, (((1,), (1,)), ((), ())), preferred_element_type=jnp.float32
    )
    dpre = (back * sigma * (1.0 + pre * (1.0 - sigma))).astype(jnp.bfloat16)
    first_bias_term = jnp.sum(dpre.astype(jnp.float32), axis=0)
    share = lax.psum_scatter(
        lax.dot_general(inputs, dpre, (((0,), (0,)), ((), ())), preferred_element_type=jnp.float32),
        "dom",
        scatter_dimension=0,
        tiled=True,
    )
    grad_first = lax.psum(share, "group")
    grad_first_bias, grad_second, grad_second_bias = lax.psum(
        (first_bias_term, second_term, second_bias_term), ("group", "dom")
    )
    return (current, grad_first, grad_first_bias, grad_second, grad_second_bias)


def solution(mesh):
    in_specs = (
        P(("group", "dom"), None),
        P(("group", "dom")),
        P(("group", "dom"), None),
        P(("group", "dom"), None),
        P(("group", "dom"), None),
        P("group", "dom", None, None),
        P("group", "dom", None, None),
        P(("group", "dom")),
        P(),
        P(),
        P(),
        P(),
    )
    out_specs = (P(("group", "dom"), None), P("dom", None), P(), P(), P())
    return jax.shard_map(local, mesh=mesh, in_specs=in_specs, out_specs=out_specs, check_vma=False)
```

profile of v0, /device:TPU:0, one launch (start us, length us, event | category | flops | bytes accessed | tf_op | source)
XLA Modules:
  0.0 363.8 jit_solution(1645723564046518858)
XLA Ops:
  13.9 4.3 %all-to-all-start.1 = ((f32[4,32,1024]{2,1,0:T(8,128)}), f32[4,32,1024]{2,1,0:T(8,128)}, u32[]{:S(2)}, u32[]{:S(2)}) async-start(f32[4,32,1024]{2,1,0:T(8,128)} %bitcast.91), calls=%async_computation.1 | async-start | bytes 1048576 | tf_op jit(solution)/shard_map/all_to_all | solution.py:17
  20.3 7.3 %all-to-all-done.1 = f32[4,32,1024]{2,1,0:T(8,128)} async-done(((f32[4,32,1024]{2,1,0:T(8,128)}), f32[4,32,1024]{2,1,0:T(8,128)}, u32[]{:S(2)}, u32[]{:S(2)}) %all-to-all-start.1) | async-done | bytes 524320 | tf_op jit(solution)/shard_map/all_to_all | solution.py:17
  27.6 6.6 %all-to-all-start = ((f32[8,32,1024]{2,1,0:T(8,128)}), f32[8,32,1024]{2,1,0:T(8,128)}, u32[]{:S(2)}, u32[]{:S(2)}) async-start(f32[8,32,1024]{2,1,0:T(8,128)} %bitcast.88), calls=%async_computation | async-start | bytes 2097152 | tf_op jit(solution)/shard_map/all_to_all | solution.py:13
  36.1 23.8 %all-to-all-done = f32[8,32,1024]{2,1,0:T(8,128)} async-done(((f32[8,32,1024]{2,1,0:T(8,128)}), f32[8,32,1024]{2,1,0:T(8,128)}, u32[]{:S(2)}, u32[]{:S(2)}) %all-to-all-start) | async-done | bytes 1048608 | tf_op jit(solution)/shard_map/all_to_all | solution.py:13
  59.9 2.2 convolution_bitcast_fusion.8
  66.1 4.1 %all-to-all-start.3 = ((f32[4,32,1024]{2,1,0:T(8,128)}), f32[4,32,1024]{2,1,0:T(8,128)}, u32[]{:S(2)}, u32[]{:S(2)}) async-start(f32[4,32,1024]{2,1,0:T(8,128)} %bitcast.93), calls=%async_computation.3 | async-start | bytes 1048576 | tf_op jit(solution)/shard_map/all_to_all | solution.py:17
  70.3 2.1 gather_fusion.2
  72.4 6.8 %all-to-all-done.3 = f32[4,32,1024]{2,1,0:T(8,128)} async-done(((f32[4,32,1024]{2,1,0:T(8,128)}), f32[4,32,1024]{2,1,0:T(8,128)}, u32[]{:S(2)}, u32[]{:S(2)}) %all-to-all-start.3) | async-done | bytes 524320 | tf_op jit(solution)/shard_map/all_to_all | solution.py:17
  79.2 4.4 %all-to-all-start.2 = ((f32[8,32,1024]{2,1,0:T(8,128)}), f32[8,32,1024]{2,1,0:T(8,128)}, u32[]{:S(2)}, u32[]{:S(2)}) async-start(f32[8,32,1024]{2,1,0:T(8,128)} %bitcast.90), calls=%async_computation.2 | async-start | bytes 2097152 | tf_op jit(solution)/shard_map/all_to_all | solution.py:13
  83.6 2.4 convolution_bitcast_fusion.2
  86.0 23.3 %all-to-all-done.2 = f32[8,32,1024]{2,1,0:T(8,128)} async-done(((f32[8,32,1024]{2,1,0:T(8,128)}), f32[8,32,1024]{2,1,0:T(8,128)}, u32[]{:S(2)}, u32[]{:S(2)}) %all-to-all-start.2) | async-done | bytes 1048608 | tf_op jit(solution)/shard_map/all_to_all | solution.py:13
  109.3 2.2 convolution_bitcast_fusion.7
  111.6 2.2 fusion.11
  116.6 4.1 %all-to-all-start.5 = ((f32[4,32,1024]{2,1,0:T(8,128)}), f32[4,32,1024]{2,1,0:T(8,128)}, u32[]{:S(2)}, u32[]{:S(2)}) async-start(f32[4,32,1024]{2,1,0:T(8,128)} %bitcast.92), calls=%async_computation.5 | async-start | bytes 1048576 | tf_op jit(solution)/shard_map/all_to_all | solution.py:17
  122.8 6.8 %all-to-all-done.5 = f32[4,32,1024]{2,1,0:T(8,128)} async-done(((f32[4,32,1024]{2,1,0:T(8,128)}), f32[4,32,1024]{2,1,0:T(8,128)}, u32[]{:S(2)}, u32[]{:S(2)}) %all-to-all-start.5) | async-done | bytes 524320 | tf_op jit(solution)/shard_map/all_to_all | solution.py:17
  129.6 4.2 %all-to-all-start.4 = ((f32[8,32,1024]{2,1,0:T(8,128)}), f32[8,32,1024]{2,1,0:T(8,128)}, u32[]{:S(2)}, u32[]{:S(2)}) async-start(f32[8,32,1024]{2,1,0:T(8,128)} %bitcast.89), calls=%async_computation.4 | async-start | bytes 2097152 | tf_op jit(solution)/shard_map/all_to_all | solution.py:13
  133.9 2.4 convolution_bitcast_fusion
  136.4 23.3 %all-to-all-done.4 = f32[8,32,1024]{2,1,0:T(8,128)} async-done(((f32[8,32,1024]{2,1,0:T(8,128)}), f32[8,32,1024]{2,1,0:T(8,128)}, u32[]{:S(2)}, u32[]{:S(2)}) %all-to-all-start.4) | async-done | bytes 1048608 | tf_op jit(solution)/shard_map/all_to_all | solution.py:13
  159.6 2.2 convolution_bitcast_fusion.6
  165.2 2.6 fusion.17
  168.8 86.5 %reduce-scatter.2.cloned.1.call-done = f32[128,1024]{1,0:T(8,128)} async-done(((f32[1024,1024]{1,0:T(8,128)}), f32[128,1024]{1,0:T(8,128)}) %reduce-scatter.2.cloned.1.call-update) | async-done | bytes 524304 | tf_op jit(solution)/shard_map/reduce_scatter | solution.py:79
  256.5 40.4 %all-reduce = (f32[1024]{0:T(1024)}, f32[19]{0:T(128)}) all-reduce(f32[1024]{0:T(1024)S(1)} %get-tuple-element.16, f32[19]{0:T(128)S(1)} %fusion.26), channel_id=1, replica_groups=mesh['group'=4,'dom'=8] {'group','dom'}, use_global_device_ids=true, to_apply=%region_8.9 | all-reduce | flops 1043 | bytes 8344 | tf_op jit(solution)/shard_map/psum | solution.py:86
  296.8 19.7 %all-reduce.6.cloned.1.call-done = f32[1024,19]{0,1:T(8,128)} async-done(((f32[1024,19]{0,1:T(8,128)}), f32[1024,19]{0,1:T(8,128)}) %all-reduce.6.cloned.1.call-update) | async-done | bytes 77840 | tf_op jit(solution)/shard_map/psum | solution.py:86
  316.6 36.4 %all-reduce.4.cloned.1.call-done = f32[128,1024]{1,0:T(8,128)} async-done(((f32[128,1024]{1,0:T(8,128)}), f32[128,1024]{1,0:T(8,128)}) %all-reduce.4.cloned.1.call-update) | async-done | bytes 524304 | tf_op jit(solution)/shard_map/psum | solution.py:85
  (60 shorter events, 27.5 us)
Async XLA Ops:
  8.0 155.8 %copy-start = (bf16[1024,1024]{1,0:T(8,128)(2,1)S(1)}, bf16[1024,1024]{1,0:T(8,128)(2,1)}, u32[]{:S(2)}) copy-start(bf16[1024,1024]{1,0:T(8,128)(2,1)} %param.20) | copy-start | bytes 6291460
  8.0 4.1 %copy-start.7 = (s32[1,1,4,32]{3,2,1,0:T(4,128)S(1)}, s32[1,1,4,32]{3,2,1,0:T(4,128)}, u32[]{:S(2)}) copy-start(s32[1,1,4,32]{3,2,1,0:T(4,128)} %param.18) | copy-start | bytes 1540
  12.3 5.9 %copy-start.5 = (s32[1,1,8,32]{3,2,1,0:T(8,128)S(1)}, s32[1,1,8,32]{3,2,1,0:T(8,128)}, u32[]{:S(2)}) copy-start(s32[1,1,8,32]{3,2,1,0:T(8,128)} %param.17) | copy-start | bytes 3076
  13.9 13.7 %all-to-all-start.1 = ((f32[4,32,1024]{2,1,0:T(8,128)}), f32[4,32,1024]{2,1,0:T(8,128)}, u32[]{:S(2)}, u32[]{:S(2)}) async-start(f32[4,32,1024]{2,1,0:T(8,128)} %bitcast.91), calls=%async_computation.1 | async-start | bytes 1048576 | tf_op jit(solution)/shard_map/all_to_all | solution.py:17
  20.3 13.9 %copy-start.2 = (bf16[128,256]{1,0:T(8,128)(2,1)S(1)}, bf16[128,256]{1,0:T(8,128)(2,1)}, u32[]{:S(2)}) copy-start(bf16[128,256]{1,0:T(8,128)(2,1)} %param.15) | copy-start | bytes 196612
  20.3 14.0 %copy-start.3 = (bf16[128,128]{1,0:T(8,128)(2,1)S(1)}, bf16[128,128]{1,0:T(8,128)(2,1)}, u32[]{:S(2)}) copy-start(bf16[128,128]{1,0:T(8,128)(2,1)} %param.16) | copy-start | bytes 98308
  20.3 14.0 %copy-start.4 = (bf16[128,128]{1,0:T(8,128)(2,1)S(1)}, bf16[128,128]{1,0:T(8,128)(2,1)}, u32[]{:S(2)}) copy-start(bf16[128,128]{1,0:T(8,128)(2,1)} %param.14) | copy-start | bytes 98308
  27.6 32.3 %all-to-all-start = ((f32[8,32,1024]{2,1,0:T(8,128)}), f32[8,32,1024]{2,1,0:T(8,128)}, u32[]{:S(2)}, u32[]{:S(2)}) async-start(f32[8,32,1024]{2,1,0:T(8,128)} %bitcast.88), calls=%async_computation | async-start | bytes 2097152 | tf_op jit(solution)/shard_map/all_to_all | solution.py:13
  66.1 13.0 %all-to-all-start.3 = ((f32[4,32,1024]{2,1,0:T(8,128)}), f32[4,32,1024]{2,1,0:T(8,128)}, u32[]{:S(2)}, u32[]{:S(2)}) async-start(f32[4,32,1024]{2,1,0:T(8,128)} %bitcast.93), calls=%async_computation.3 | async-start | bytes 1048576 | tf_op jit(solution)/shard_map/all_to_all | solution.py:17
  79.2 32.4 %copy-start.1 = (f32[128,1024]{0,1:T(8,128)S(1)}, f32[128,1024]{0,1:T(8,128)}, u32[]{:S(2)}) copy-start(f32[128,1024]{0,1:T(8,128)} %fusion.7) | copy-start | bytes 1572868
  79.2 30.1 %all-to-all-start.2 = ((f32[8,32,1024]{2,1,0:T(8,128)}), f32[8,32,1024]{2,1,0:T(8,128)}, u32[]{:S(2)}, u32[]{:S(2)}) async-start(f32[8,32,1024]{2,1,0:T(8,128)} %bitcast.90), calls=%async_computation.2 | async-start | bytes 2097152 | tf_op jit(solution)/shard_map/all_to_all | solution.py:13
  116.6 13.0 %all-to-all-start.5 = ((f32[4,32,1024]{2,1,0:T(8,128)}), f32[4,32,1024]{2,1,0:T(8,128)}, u32[]{:S(2)}, u32[]{:S(2)}) async-start(f32[4,32,1024]{2,1,0:T(8,128)} %bitcast.92), calls=%async_computation.5 | async-start | bytes 1048576 | tf_op jit(solution)/shard_map/all_to_all | solution.py:17
  129.6 30.0 %all-to-all-start.4 = ((f32[8,32,1024]{2,1,0:T(8,128)}), f32[8,32,1024]{2,1,0:T(8,128)}, u32[]{:S(2)}, u32[]{:S(2)}) async-start(f32[8,32,1024]{2,1,0:T(8,128)} %bitcast.89), calls=%async_computation.4 | async-start | bytes 2097152 | tf_op jit(solution)/shard_map/all_to_all | solution.py:13
  133.9 121.4 %reduce-scatter.2.cloned.1.call-start = ((), (), s32[]{:S(2)}) async-start(), calls=%async_computation.7 | async-start | bytes 4718592 | tf_op jit(solution)/shard_map/reduce_scatter | solution.py:79
  159.6 4.1 %copy-start.9 = (f32[1024]{0:T(1024)S(1)}, f32[1024]{0:T(1024)}, u32[]{:S(2)}) copy-start(f32[1024]{0:T(1024)} %param.21) | copy-start | bytes 12292
  163.8 0.8 copy-start.8
  163.8 0.8 copy-start.10
  163.8 1.0 copy-start.6
  167.8 148.7 %all-reduce.6.cloned.1.call-start = ((), (), s32[]{:S(2)}) async-start(), calls=%async_computation.9 | async-start | bytes 196608 | tf_op jit(solution)/shard_map/psum | solution.py:86
  168.7 184.3 %all-reduce.4.cloned.1.call-start = ((), (), s32[]{:S(2)}) async-start(), calls=%async_computation.8 | async-start | bytes 1048576 | tf_op jit(solution)/shard_map/psum | solution.py:85
Sparse Core Ops, SparseCore 0:
  168.0 87.3 reduce-scatter.1
Sparse Core Ops, SparseCore 1:
  174.5 142.0 all-reduce.5
  318.8 34.2 all-reduce.3
where the time goes:
time: 365 us; the launch traced here: 364 us
  waiting for transfers between devices  234 us (64%)
  blocking collectives  40.4 us (11%)
  starting transfers between devices  27.9 us (8%)
  matrix products  23 us (6%)
  local copies, waits for them, and re-layouts  20.8 us (6%)
  between operations  15.7 us (4%)
    reduce_scatter x1, waiting for transfers between devices, local(): lax.psum_scatter(lax.dot_general(inputs, dpre, (((0,), (0,)), ((), ())),...  86.5 us
    all_to_all x3, waiting for transfers between devices, fetch_halos(): lax.all_to_all(outgoing, 'dom', split_axis=0, concat_axis=0, tiled=True)  70.4 us
    psum x1, blocking collectives, local(): lax.psum((first_bias_term, second_term, second_bias_term), ('group', 'dom'))  40.4 us
    psum x1, waiting for transfers between devices, local(): grad_first = lax.psum(share, 'group')  36.4 us
    all_to_all x3, waiting for transfers between devices, fetch_halos(): lax.all_to_all(leaving, 'group', split_axis=0, concat_axis=0, tiled=True)  20.9 us
    psum x1, waiting for transfers between devices, local(): lax.psum((first_bias_term, second_term, second_bias_term), ('group', 'dom'))  19.7 us
    all_to_all x3, starting transfers between devices, fetch_halos(): lax.all_to_all(outgoing, 'dom', split_axis=0, concat_axis=0, tiled=True)  15.2 us
    all_to_all x3, starting transfers between devices, fetch_halos(): lax.all_to_all(leaving, 'group', split_axis=0, concat_axis=0, tiled=True)  12.6 us
  transfers between devices with their start and end apart: 9, of which 9 were waited for; matrix products, arithmetic and copies ran while one was open for 4% of the time, Pallas kernels for 0%

commit v1 on v0

--- a/solution.py
+++ b/solution.py
@@ -84,7 +84,7 @@
     )
     grad_first = lax.psum(share, "group")
     grad_first_bias, grad_second, grad_second_bias = lax.psum(
-        (first_bias_term, second_term, second_bias_term), ("group", "dom")
+        lax.psum((first_bias_term, second_term, second_bias_term), "dom"), "group"
     )
     return (current, grad_first, grad_first_bias, grad_second, grad_second_bias)
 

time: 365 us -> 375 us (1.027)
  waiting for transfers between devices: 234 us -> 256 us
  blocking collectives: 40.4 us -> 26.7 us
    psum x1, waiting for transfers between devices: 19.7 us -> 65.9 us  [local(): lax.psum((first_bias_term, second_term, second_bias_term), 'dom')]
    psum x1, waiting for transfers between devices: 36.4 us -> 8.33 us  [local(): grad_first = lax.psum(share, 'group')]
    psum x1 -> x2, blocking collectives: 40.4 us -> 26.7 us  [the longest x1 20.3 us: local(): lax.psum((first_bias_term, second_term, second_bias_term), 'dom')]
    reduce_scatter x1, waiting for transfers between devices: 86.5 us -> 91 us  [local(): lax.psum_scatter(lax.dot_general(inputs, dpre, (((0,), (0,)), ((), ())),...]
  transfers between devices with their start and end apart: 9 -> 9, of which waited for: 9 -> 9; matrix products, arithmetic and copies ran while one was open for 4% -> 5% of each run, Pallas kernels for 0% -> 0%
where the time goes in v1:
time: 375 us; the launch traced here: 373 us
  waiting for transfers between devices  256 us (68%)
  starting transfers between devices  27.9 us (7%)
  matrix products  26.7 us (7%)
  blocking collectives  26.7 us (7%)
  local copies, waits for them, and re-layouts  20.6 us (5%)
  between operations  14 us (4%)
    reduce_scatter x1, waiting for transfers between devices, local(): lax.psum_scatter(lax.dot_general(inputs, dpre, (((0,), (0,)), ((), ())),...  91 us
    all_to_all x3, waiting for transfers between devices, fetch_halos(): lax.all_to_all(outgoing, 'dom', split_axis=0, concat_axis=0, tiled=True)  69.6 us
    psum x1, waiting for transfers between devices, local(): lax.psum((first_bias_term, second_term, second_bias_term), 'dom')  65.9 us
    all_to_all x3, waiting for transfers between devices, fetch_halos(): lax.all_to_all(leaving, 'group', split_axis=0, concat_axis=0, tiled=True)  20.9 us
    psum x1, blocking collectives, local(): lax.psum((first_bias_term, second_term, second_bias_term), 'dom')  20.3 us
    all_to_all x3, starting transfers between devices, fetch_halos(): lax.all_to_all(outgoing, 'dom', split_axis=0, concat_axis=0, tiled=True)  15.2 us
    all_to_all x3, starting transfers between devices, fetch_halos(): lax.all_to_all(leaving, 'group', split_axis=0, concat_axis=0, tiled=True)  12.6 us
    psum x1, waiting for transfers between devices, local(): grad_first = lax.psum(share, 'group')  8.33 us
  transfers between devices with their start and end apart: 9, of which 9 were waited for; matrix products, arithmetic and copies ran while one was open for 5% of the time, Pallas kernels for 0%

profile of v1, /device:TPU:0, one launch (start us, length us, event | category | flops | bytes accessed | tf_op | source)
XLA Modules:
  0.0 373.5 jit_solution(5187540699370002483)
XLA Ops:
  13.0 4.3 %all-to-all-start.1 = ((f32[4,32,1024]{2,1,0:T(8,128)}), f32[4,32,1024]{2,1,0:T(8,128)}, u32[]{:S(2)}, u32[]{:S(2)}) async-start(f32[4,32,1024]{2,1,0:T(8,128)} %bitcast.91), calls=%async_computation.1 | async-start | bytes 1048576 | tf_op jit(solution)/shard_map/all_to_all | solution.py:17
  19.5 7.3 %all-to-all-done.1 = f32[4,32,1024]{2,1,0:T(8,128)} async-done(((f32[4,32,1024]{2,1,0:T(8,128)}), f32[4,32,1024]{2,1,0:T(8,128)}, u32[]{:S(2)}, u32[]{:S(2)}) %all-to-all-start.1) | async-done | bytes 524320 | tf_op jit(solution)/shard_map/all_to_all | solution.py:17
  26.7 6.6 %all-to-all-start = ((f32[8,32,1024]{2,1,0:T(8,128)}), f32[8,32,1024]{2,1,0:T(8,128)}, u32[]{:S(2)}, u32[]{:S(2)}) async-start(f32[8,32,1024]{2,1,0:T(8,128)} %bitcast.88), calls=%async_computation | async-start | bytes 2097152 | tf_op jit(solution)/shard_map/all_to_all | solution.py:13
  33.6 2.4 convolution_bitcast_fusion.4
  36.0 23.0 %all-to-all-done = f32[8,32,1024]{2,1,0:T(8,128)} async-done(((f32[8,32,1024]{2,1,0:T(8,128)}), f32[8,32,1024]{2,1,0:T(8,128)}, u32[]{:S(2)}, u32[]{:S(2)}) %all-to-all-start) | async-done | bytes 1048608 | tf_op jit(solution)/shard_map/all_to_all | solution.py:13
  59.0 2.2 convolution_bitcast_fusion.8
  61.3 2.3 fusion.7
  66.4 4.1 %all-to-all-start.3 = ((f32[4,32,1024]{2,1,0:T(8,128)}), f32[4,32,1024]{2,1,0:T(8,128)}, u32[]{:S(2)}, u32[]{:S(2)}) async-start(f32[4,32,1024]{2,1,0:T(8,128)} %bitcast.93), calls=%async_computation.3 | async-start | bytes 1048576 | tf_op jit(solution)/shard_map/all_to_all | solution.py:17
  72.6 6.8 %all-to-all-done.3 = f32[4,32,1024]{2,1,0:T(8,128)} async-done(((f32[4,32,1024]{2,1,0:T(8,128)}), f32[4,32,1024]{2,1,0:T(8,128)}, u32[]{:S(2)}, u32[]{:S(2)}) %all-to-all-start.3) | async-done | bytes 524320 | tf_op jit(solution)/shard_map/all_to_all | solution.py:17
  79.4 4.4 %all-to-all-start.2 = ((f32[8,32,1024]{2,1,0:T(8,128)}), f32[8,32,1024]{2,1,0:T(8,128)}, u32[]{:S(2)}, u32[]{:S(2)}) async-start(f32[8,32,1024]{2,1,0:T(8,128)} %bitcast.90), calls=%async_computation.2 | async-start | bytes 2097152 | tf_op jit(solution)/shard_map/all_to_all | solution.py:13
  83.8 2.4 convolution_bitcast_fusion.2
  86.2 23.3 %all-to-all-done.2 = f32[8,32,1024]{2,1,0:T(8,128)} async-done(((f32[8,32,1024]{2,1,0:T(8,128)}), f32[8,32,1024]{2,1,0:T(8,128)}, u32[]{:S(2)}, u32[]{:S(2)}) %all-to-all-start.2) | async-done | bytes 1048608 | tf_op jit(solution)/shard_map/all_to_all | solution.py:13
  116.8 4.1 %all-to-all-start.5 = ((f32[4,32,1024]{2,1,0:T(8,128)}), f32[4,32,1024]{2,1,0:T(8,128)}, u32[]{:S(2)}, u32[]{:S(2)}) async-start(f32[4,32,1024]{2,1,0:T(8,128)} %bitcast.92), calls=%async_computation.5 | async-start | bytes 1048576 | tf_op jit(solution)/shard_map/all_to_all | solution.py:17
  123.0 6.8 %all-to-all-done.5 = f32[4,32,1024]{2,1,0:T(8,128)} async-done(((f32[4,32,1024]{2,1,0:T(8,128)}), f32[4,32,1024]{2,1,0:T(8,128)}, u32[]{:S(2)}, u32[]{:S(2)}) %all-to-all-start.5) | async-done | bytes 524320 | tf_op jit(solution)/shard_map/all_to_all | solution.py:17
  129.9 4.2 %all-to-all-start.4 = ((f32[8,32,1024]{2,1,0:T(8,128)}), f32[8,32,1024]{2,1,0:T(8,128)}, u32[]{:S(2)}, u32[]{:S(2)}) async-start(f32[8,32,1024]{2,1,0:T(8,128)} %bitcast.89), calls=%async_computation.4 | async-start | bytes 2097152 | tf_op jit(solution)/shard_map/all_to_all | solution.py:13
  134.2 2.4 convolution_bitcast_fusion
  136.6 23.3 %all-to-all-done.4 = f32[8,32,1024]{2,1,0:T(8,128)} async-done(((f32[8,32,1024]{2,1,0:T(8,128)}), f32[8,32,1024]{2,1,0:T(8,128)}, u32[]{:S(2)}, u32[]{:S(2)}) %all-to-all-start.4) | async-done | bytes 1048608 | tf_op jit(solution)/shard_map/all_to_all | solution.py:13
  159.9 2.2 convolution_bitcast_fusion.6
  167.8 2.6 fusion.17
  170.5 65.9 %all-reduce.6.cloned.1.call-done = f32[1024,19]{0,1:T(8,128)} async-done(((f32[1024,19]{0,1:T(8,128)}), f32[1024,19]{0,1:T(8,128)}) %all-reduce.6.cloned.1.call-update) | async-done | bytes 77840 | tf_op jit(solution)/shard_map/psum | solution.py:87
  236.4 91.0 %reduce-scatter.2.cloned.1.call-done = f32[128,1024]{1,0:T(8,128)} async-done(((f32[1024,1024]{1,0:T(8,128)}), f32[128,1024]{1,0:T(8,128)}) %reduce-scatter.2.cloned.1.call-update) | async-done | bytes 524304 | tf_op jit(solution)/shard_map/reduce_scatter | solution.py:79
  328.5 20.3 %all-reduce = (f32[1024]{0:T(1024)S(1)}, f32[19]{0:T(128)S(1)}) all-reduce(f32[1024]{0:T(1024)S(1)} %get-tuple-element.20, f32[19]{0:T(128)S(1)} %fusion.26), channel_id=1, replica_groups=mesh['group'=4,'dom'=8] {'dom'}, use_global_device_ids=true, to_apply=%region_8.9 | all-reduce | flops 1043 | bytes 8344 | tf_op jit(solution)/shard_map/psum | solution.py:87
  348.8 6.3 %all-reduce.1 = (f32[1024]{0:T(1024)}, f32[19]{0:T(128)}) all-reduce(f32[1024]{0:T(1024)S(1)} %get-tuple-element.10, f32[19]{0:T(128)S(1)} %get-tuple-element.11), channel_id=1, replica_groups=mesh['group'=4,'dom'=8] {'group'}, use_global_device_ids=true, to_apply=%region_9.10 | all-reduce | flops 1043 | bytes 8344 | tf_op jit(solution)/shard_map/psum | solution.py:86
  355.2 8.3 %all-reduce.8.cloned.1.call-done = (f32[128,1024]{1,0:T(8,128)}, f32[1024,19]{0,1:T(8,128)}) async-done(((f32[128,1024]{1,0:T(8,128)}, f32[1024,19]{0,1:T(8,128)}), (f32[128,1024]{1,0:T(8,128)}, f32[1024,19]{0,1:T(8,128)})) %all-reduce.8.cloned.1.call-update) | async-done | bytes 602128 | tf_op jit(solution)/shard_map/psum | solution.py:85
  (61 shorter events, 32.7 us)
Async XLA Ops:
  7.2 156.8 %copy-start = (bf16[1024,1024]{1,0:T(8,128)(2,1)S(1)}, bf16[1024,1024]{1,0:T(8,128)(2,1)}, u32[]{:S(2)}) copy-start(bf16[1024,1024]{1,0:T(8,128)(2,1)} %param.20) | copy-start | bytes 6291460
  7.2 4.1 %copy-start.7 = (s32[1,1,4,32]{3,2,1,0:T(4,128)S(1)}, s32[1,1,4,32]{3,2,1,0:T(4,128)}, u32[]{:S(2)}) copy-start(s32[1,1,4,32]{3,2,1,0:T(4,128)} %param.18) | copy-start | bytes 1540
  11.4 5.9 %copy-start.5 = (s32[1,1,8,32]{3,2,1,0:T(8,128)S(1)}, s32[1,1,8,32]{3,2,1,0:T(8,128)}, u32[]{:S(2)}) copy-start(s32[1,1,8,32]{3,2,1,0:T(8,128)} %param.17) | copy-start | bytes 3076
  13.0 13.7 %all-to-all-start.1 = ((f32[4,32,1024]{2,1,0:T(8,128)}), f32[4,32,1024]{2,1,0:T(8,128)}, u32[]{:S(2)}, u32[]{:S(2)}) async-start(f32[4,32,1024]{2,1,0:T(8,128)} %bitcast.91), calls=%async_computation.1 | async-start | bytes 1048576 | tf_op jit(solution)/shard_map/all_to_all | solution.py:17
  19.4 13.9 %copy-start.2 = (bf16[128,256]{1,0:T(8,128)(2,1)S(1)}, bf16[128,256]{1,0:T(8,128)(2,1)}, u32[]{:S(2)}) copy-start(bf16[128,256]{1,0:T(8,128)(2,1)} %param.15) | copy-start | bytes 196612
  19.4 14.0 %copy-start.3 = (bf16[128,128]{1,0:T(8,128)(2,1)S(1)}, bf16[128,128]{1,0:T(8,128)(2,1)}, u32[]{:S(2)}) copy-start(bf16[128,128]{1,0:T(8,128)(2,1)} %param.16) | copy-start | bytes 98308
  19.4 14.0 %copy-start.4 = (bf16[128,128]{1,0:T(8,128)(2,1)S(1)}, bf16[128,128]{1,0:T(8,128)(2,1)}, u32[]{:S(2)}) copy-start(bf16[128,128]{1,0:T(8,128)(2,1)} %param.14) | copy-start | bytes 98308
  26.7 32.3 %all-to-all-start = ((f32[8,32,1024]{2,1,0:T(8,128)}), f32[8,32,1024]{2,1,0:T(8,128)}, u32[]{:S(2)}, u32[]{:S(2)}) async-start(f32[8,32,1024]{2,1,0:T(8,128)} %bitcast.88), calls=%async_computation | async-start | bytes 2097152 | tf_op jit(solution)/shard_map/all_to_all | solution.py:13
  66.4 13.0 %all-to-all-start.3 = ((f32[4,32,1024]{2,1,0:T(8,128)}), f32[4,32,1024]{2,1,0:T(8,128)}, u32[]{:S(2)}, u32[]{:S(2)}) async-start(f32[4,32,1024]{2,1,0:T(8,128)} %bitcast.93), calls=%async_computation.3 | async-start | bytes 1048576 | tf_op jit(solution)/shard_map/all_to_all | solution.py:17
  79.4 32.4 %copy-start.1 = (f32[128,1024]{0,1:T(8,128)S(1)}, f32[128,1024]{0,1:T(8,128)}, u32[]{:S(2)}) copy-start(f32[128,1024]{0,1:T(8,128)} %fusion.7) | copy-start | bytes 1572868
  79.4 30.1 %all-to-all-start.2 = ((f32[8,32,1024]{2,1,0:T(8,128)}), f32[8,32,1024]{2,1,0:T(8,128)}, u32[]{:S(2)}, u32[]{:S(2)}) async-start(f32[8,32,1024]{2,1,0:T(8,128)} %bitcast.90), calls=%async_computation.2 | async-start | bytes 2097152 | tf_op jit(solution)/shard_map/all_to_all | solution.py:13
  116.8 13.0 %all-to-all-start.5 = ((f32[4,32,1024]{2,1,0:T(8,128)}), f32[4,32,1024]{2,1,0:T(8,128)}, u32[]{:S(2)}, u32[]{:S(2)}) async-start(f32[4,32,1024]{2,1,0:T(8,128)} %bitcast.92), calls=%async_computation.5 | async-start | bytes 1048576 | tf_op jit(solution)/shard_map/all_to_all | solution.py:17
  129.9 30.0 %all-to-all-start.4 = ((f32[8,32,1024]{2,1,0:T(8,128)}), f32[8,32,1024]{2,1,0:T(8,128)}, u32[]{:S(2)}, u32[]{:S(2)}) async-start(f32[8,32,1024]{2,1,0:T(8,128)} %bitcast.89), calls=%async_computation.4 | async-start | bytes 2097152 | tf_op jit(solution)/shard_map/all_to_all | solution.py:13
  134.1 102.3 %all-reduce.6.cloned.1.call-start = ((), (), s32[]{:S(2)}) async-start(), calls=%async_computation.8 | async-start | bytes 196608 | tf_op jit(solution)/shard_map/psum | solution.py:87
  159.8 4.1 %copy-start.9 = (f32[1024]{0:T(1024)S(1)}, f32[1024]{0:T(1024)}, u32[]{:S(2)}) copy-start(f32[1024]{0:T(1024)} %param.21) | copy-start | bytes 12292
  164.0 1.3 copy-start.8
  164.0 1.3 copy-start.10
  164.0 1.5 copy-start.6
  167.8 159.6 %reduce-scatter.2.cloned.1.call-start = ((), (), s32[]{:S(2)}) async-start(), calls=%async_computation.7 | async-start | bytes 4718592 | tf_op jit(solution)/shard_map/reduce_scatter | solution.py:79
  170.5 193.0 %all-reduce.8.cloned.1.call-start = ((), (), s32[]{:S(2)}) async-start(), calls=%async_computation.9 | async-start | bytes 1245184 | tf_op jit(solution)/shard_map/psum | solution.py:85
Sparse Core Ops, SparseCore 0:
  167.9 68.4 all-reduce.5
  240.0 87.3 reduce-scatter.1
  329.9 33.5 all-reduce.7
